TPU v7x, 32 devices: a whole 2x2x4 slice. The times are simulated.
32 devices in a mesh: replica: 4 (over y, x), fsdp: 8 (over z, core).
Axes of the slice: x: 2, y: 2, z: 4, core: 2. Of those that a mesh axis runs over, the one named last changes fastest.
Arguments:
- local_weights: bfloat16 [4, 256, 28672], P('replica', 'fsdp'), may hold values from -6 to 6
- base_weights: float32 [256, 28672], P('fsdp'), may hold values from -6 to 6
- momentum: float32 [256, 28672], P('replica', 'fsdp'), may hold values from -4 to 4
Outputs:
- new_weights: float32 [256, 28672], P('fsdp')
- new_momentum: float32 [256, 28672], P('replica', 'fsdp')
All inputs are finite; a program needn't handle non-finite values. Where the computation divides by a largest or mean magnitude, that divisor is 1e-20 or more.
Results may differ from a plain program's by a relative error of at most 0.015.
Values may be sent and summed in bfloat16 or wider, within the bound.
A program may use at most 128 MiB of HBM per device.

v0:
```python
import jax
import jax.numpy as jnp
from jax import lax
from jax.sharding import PartitionSpec as P

QBLOCK = 128
EPSILON = 1e-06
LEARN_RATE = 0.7
MOMENTUM_COEF = 0.9


def dequantise(integer_levels, block_scales):
    shaped = integer_levels.astype(jnp.float32).reshape(block_scales.shape + (QBLOCK,))
    values = shaped * block_scales.astype(jnp.float32)[..., None]
    return values.reshape(integer_levels.shape)


def per_device(local_weights, base_weights, momentum):
    row_count, col_count = base_weights.shape
    replica_differences = base_weights - local_weights[0].astype(jnp.float32)
    block_grouped = replica_differences.reshape(row_count, col_count // QBLOCK, QBLOCK)
    block_scales = (jnp.max(jnp.abs(block_grouped), axis=2) + EPSILON).astype(jnp.bfloat16)
    integer_levels = (block_grouped / block_scales.astype(jnp.float32)[:, :, None]).astype(
        jnp.bfloat16
    )
    levels_local = integer_levels.reshape(1, row_count, col_count)
    scales_local = block_scales.reshape(1, row_count, col_count // QBLOCK)
    replica_count = lax.axis_size("replica")
    shard_group_count = lax.axis_size("fsdp")
    group = shard_group_count // replica_count
    piece = momentum.shape[1] // shard_group_count
    levels_owned, scales_owned = (
        lax.all_to_all(levels_local, "replica", split_axis=2, concat_axis=0, tiled=True),
        lax.all_to_all(scales_local, "replica", split_axis=2, concat_axis=0, tiled=True),
    )
    summed = jnp.sum(dequantise(levels_owned, scales_owned), axis=0)
    sectioned = momentum.reshape(group, row_count, shard_group_count, piece)
    sectioned = lax.all_to_all(sectioned, "fsdp", split_axis=2, concat_axis=2, tiled=True)
    sectioned = lax.all_to_all(sectioned, "replica", split_axis=2, concat_axis=0, tiled=True)
    sectioned = lax.all_to_all(sectioned, "fsdp", split_axis=0, concat_axis=3, tiled=True)
    owned_momentum = sectioned.reshape(row_count, col_count // replica_count)
    average = summed / replica_count
    owned_new = MOMENTUM_COEF * owned_momentum + average
    update = (LEARN_RATE * (average + MOMENTUM_COEF * owned_new)).astype(jnp.bfloat16)
    returned = lax.all_gather(update, "replica", axis=1, tiled=True)
    going = owned_new.reshape(1, row_count, group, shard_group_count * piece)
    going = lax.all_to_all(going, "fsdp", split_axis=3, concat_axis=0, tiled=True)
    going = lax.all_to_all(going, "replica", split_axis=0, concat_axis=2, tiled=True)
    going = lax.all_to_all(going, "fsdp", split_axis=2, concat_axis=2, tiled=True)
    new_momentum = going.reshape(momentum.shape)
    new_weights = base_weights - returned.astype(jnp.float32)
    return (new_weights, new_momentum)


def solution(mesh):
    return jax.shard_map(
        per_device,
        mesh=mesh,
        in_specs=(P("replica", "fsdp", None), P("fsdp", None), P("replica", "fsdp")),
        out_specs=(P("fsdp", None), P("replica", "fsdp")),
        check_vma=False,
    )
```

profile of v0, /device:TPU:0, one launch (start us, length us, event | category | flops | bytes accessed | tf_op | source)
XLA Modules:
  0.0 445.3 jit_solution(15897536443774673228)
XLA Ops:
  7.2 3.0 abs_bitcast_fusion
  10.2 2.5 copy.72
  12.6 0.0 copy-start.1
  12.6 3.3 reduce_max.9
  16.0 0.1 copy.57
  16.1 0.5 broadcast.56
  16.6 1.0 reduce.3
  17.6 0.7 reshape.110
  18.3 5.2 %all-to-all-start.1 = ((bf16[4,2,896]{2,1,0:T(2,128)(2,1)}), bf16[4,2,896]{2,1,0:T(2,128)(2,1)S(1)}, u32[]{:S(2)}, u32[]{:S(2)}) async-start(bf16[4,2,896]{2,1,0:T(2,128)(2,1)} %reshape.110), calls=%async_computation.1 | async-start | bytes 28672 | tf_op jit(solution)/shard_map/all_to_all | solution.py:34
  23.5 0.0 copy-start
  23.5 1.0 div.20
  24.5 0.0 copy-done.1
  24.5 1.0 copy-done
  25.5 3.6 fusion.2
  29.1 27.0 %copy.56 = bf16[1,32,28672]{1,0,2:T(2,128)(2,1)} copy(bf16[1,32,28672]{2,1,0:T(8,128)(2,1)} %fusion.2) | data formatting | bytes 3670016 | tf_op jit(solution)/shard_map/convert_element_type | solution.py:23
  56.1 157.0 %reduce.2 = bf16[28672,32]{1,0:T(8,128)(2,1)} reduce(bf16[28672,1,32]{2,1,0:T(2,128)(2,1)} %bitcast.64, bf16[]{:T(256)} %broadcast.56), dimensions={1}, to_apply=%bitcast.56.reduce_sub_computation | reduce | bytes 3670018
  213.2 9.4 %reshape.108 = bf16[4,2,114688]{2,1,0:T(2,128)(2,1)} reshape(bf16[28672,32]{1,0:T(8,128)(2,1)} %reduce.2) | data formatting | bytes 3670016
  222.6 0.0 copy-start.2
  222.6 0.0 all-to-all-done.1
  222.6 4.3 all-to-all-start
  226.9 0.0 copy-done.2
  226.9 1.5 reshape.102
  228.4 1.8 copy.59
  230.2 18.3 %all-to-all-done = bf16[4,2,114688]{2,1,0:T(2,128)(2,1)S(1)} async-done(((bf16[4,2,114688]{2,1,0:T(2,128)(2,1)}), bf16[4,2,114688]{2,1,0:T(2,128)(2,1)S(1)}, u32[]{:S(2)}, u32[]{:S(2)}) %all-to-all-start) | async-done | bytes 1835040 | tf_op jit(solution)/shard_map/all_to_all | solution.py:33
  248.5 31.3 %all_to_all.91 = f32[2,32,8,448]{3,1,0,2:T(8,128)} all-to-all(f32[2,32,8,448]{3,1,0,2:T(8,128)S(1)} %copy.59), channel_id=1, replica_groups=mesh['replica'=4,'fsdp'=8] {'fsdp'}, dimensions={2} | all-to-all | bytes 1835008 | tf_op jit(solution)/shard_map/all_to_all | solution.py:38
  279.9 3.5 all-to-all-start.3
  283.4 0.1 reshape.111
  283.5 0.1 bitcast_convert_fusion.1
  283.6 8.1 %reshape.109 = bf16[28672,1,32]{2,1,0:T(2,128)(2,1)} reshape(bf16[4,2,114688]{2,1,0:T(2,128)(2,1)S(1)} %all-to-all-done) | data formatting | bytes 3670016
  291.8 5.1 %all-to-all-done.3 = f32[2,32,8,448]{3,1,0,2:T(8,128)S(1)} async-done(((f32[2,32,8,448]{3,1,0,2:T(8,128)}), f32[2,32,8,448]{3,1,0,2:T(8,128)S(1)}, u32[]{:S(2)}, u32[]{:S(2)}) %all-to-all-start.3) | async-done | bytes 917536 | tf_op jit(solution)/shard_map/all_to_all | solution.py:39
  296.9 1.8 copy.60
  298.8 3.6 all-to-all-start.4
  302.3 0.0 all-gather.2.cloned.1.call-start
  302.4 17.6 %bitcast_convert_fusion = f32[1,32,28672]{1,0,2:T(1,128)} fusion(bf16[28672,1,32]{2,1,0:T(2,128)(2,1)} %reshape.109), kind=kLoop, calls=%fused_computation.15 | loop fusion | flops 917504 | bytes 5505024 | tf_op jit(solution)/shard_map/convert_element_type | solution.py:13
  319.9 8.9 %fusion = f32[32,7168]{0,1:T(8,128)} fusion(f32[4,1,32,7168]{2,3,0,1:T(8,128)} %bitcast.65, f32[4,32,56]{1,2,0:T(8,128)S(1)} %bitcast.76), kind=kLoop, calls=%fused_computation.1 | loop fusion | flops 1605632 | bytes 4616192 | tf_op jit(solution)/shard_map/reduce_sum | solution.py:36
  328.8 3.3 copy.58
  332.2 0.0 all-to-all-done.4
  332.2 0.5 multiply_bitcast_fusion
  332.7 0.6 copy.61
  333.3 0.6 copy.62
  334.0 0.4 mul.52
  334.4 2.2 broadcast_multiply_fusion
  336.5 0.8 div.25
  337.3 0.4 mul.56
  337.7 0.0 all-gather.2.cloned.1.call-update
  337.8 0.2 copy_add_fusion
  338.0 3.6 copy.64
  341.6 5.2 %reshape.112 = f32[8,1,28672]{2,1,0:T(1,128)S(1)} reshape(f32[3584,1,2,32]{3,2,1,0:T(2,128)} %bitcast.67) | data formatting | bytes 1835008
  346.8 28.5 %all_to_all.92 = f32[8,1,28672]{2,1,0:T(1,128)S(1)} all-to-all(f32[8,1,28672]{2,1,0:T(1,128)S(1)} %reshape.112), channel_id=1, replica_groups=mesh['replica'=4,'fsdp'=8] {'fsdp'}, dimensions={0} | all-to-all | bytes 1835008 | tf_op jit(solution)/shard_map/all_to_all | solution.py:47
  375.3 0.5 broadcast.58
  375.8 2.8 reduce.4
  378.6 4.9 %reshape.113 = f32[3584,1,2,32]{3,2,1,0:T(2,128)} reshape(f32[8,28672]{1,0:T(8,128)S(1)} %reduce.4) | data formatting | bytes 1835008
  383.6 5.0 %copy.71 = f32[1,32,2,8,448]{4,1,2,3,0:T(8,128)S(1)} copy(f32[1,32,2,8,448]{1,2,4,3,0:T(2,128)} %bitcast.68) | data formatting | bytes 1835008 | tf_op jit(solution)/shard_map/all_to_all | solution.py:47
  388.6 16.7 %all_to_all.93 = f32[8,32,2,448]{3,1,2,0:T(8,128)S(1)} all-to-all(f32[8,32,2,448]{3,1,2,0:T(8,128)S(1)} %bitcast.74), channel_id=1, replica_groups=mesh['replica'=4,'fsdp'=8] {'replica'}, dimensions={0} | all-to-all | bytes 1835008 | tf_op jit(solution)/shard_map/all_to_all | solution.py:48
  405.3 0.1 copy.67
  405.4 1.1 copy.68
  406.4 3.6 all-to-all-start.7
  410.0 0.0 all-gather.2.cloned.1.call-done
  410.0 4.8 %convert_subtract_fusion.1 = f32[32,28672]{1,0:T(8,128)} fusion(f32[32,28672]{1,0:T(8,128)} %param.4, bf16[32,28672]{1,0:T(8,128)(2,1)} %all-gather.2.cloned.1.call-done), kind=kLoop, calls=%fused_computation.5 | loop fusion | flops 1835008 | bytes 9175040 | tf_op jit(solution)/shard_map/sub | solution.py:51
  414.8 21.7 %all-to-all-done.7 = f32[2,32,8,448]{3,1,0,2:T(8,128)S(1)} async-done(((f32[2,32,8,448]{3,1,0,2:T(8,128)}), f32[2,32,8,448]{3,1,0,2:T(8,128)S(1)}, u32[]{:S(2)}, u32[]{:S(2)}) %all-to-all-start.7) | async-done | bytes 917536 | tf_op jit(solution)/shard_map/all_to_all | solution.py:49
  436.5 0.6 copy.69
  437.1 1.3 reshape.103
  (1 shorter events, 0.0 us)
Async XLA Ops:
  12.6 11.9 %copy-start.1 = (bf16[1,32,28672]{2,1,0:T(8,128)(2,1)S(1)}, bf16[1,32,28672]{2,1,0:T(8,128)(2,1)}, u32[]{:S(2)}) copy-start(bf16[1,32,28672]{2,1,0:T(8,128)(2,1)} %param.3) | copy-start | bytes 5505028
  18.3 204.3 %all-to-all-start.1 = ((bf16[4,2,896]{2,1,0:T(2,128)(2,1)}), bf16[4,2,896]{2,1,0:T(2,128)(2,1)S(1)}, u32[]{:S(2)}, u32[]{:S(2)}) async-start(bf16[4,2,896]{2,1,0:T(2,128)(2,1)} %reshape.110), calls=%async_computation.1 | async-start | bytes 28672 | tf_op jit(solution)/shard_map/all_to_all | solution.py:34
  23.5 2.0 copy-start
  222.6 4.3 copy-start.2
  222.6 26.0 %all-to-all-start = ((bf16[4,2,114688]{2,1,0:T(2,128)(2,1)}), bf16[4,2,114688]{2,1,0:T(2,128)(2,1)S(1)}, u32[]{:S(2)}, u32[]{:S(2)}) async-start(bf16[4,2,114688]{2,1,0:T(2,128)(2,1)} %reshape.108), calls=%async_computation | async-start | bytes 3670016 | tf_op jit(solution)/shard_map/all_to_all | solution.py:33
  279.9 17.0 %all-to-all-start.3 = ((f32[2,32,8,448]{3,1,0,2:T(8,128)}), f32[2,32,8,448]{3,1,0,2:T(8,128)S(1)}, u32[]{:S(2)}, u32[]{:S(2)}) async-start(f32[2,32,8,448]{3,1,0,2:T(8,128)} %all_to_all.91), calls=%async_computation.3 | async-start | bytes 2097152 | tf_op jit(solution)/shard_map/all_to_all | solution.py:39
  298.8 33.4 %all-to-all-start.4 = ((f32[8,32,2,448]{3,2,1,0:T(2,128)}), f32[8,32,2,448]{3,2,1,0:T(2,128)S(1)}, u32[]{:S(2)}, u32[]{:S(2)}) async-start(f32[8,32,2,448]{3,2,1,0:T(2,128)} %bitcast.71), calls=%async_computation.4 | async-start | bytes 2097152 | tf_op jit(solution)/shard_map/all_to_all | solution.py:40
  302.3 107.7 %all-gather.2.cloned.1.call-start = ((), (), s32[]{:S(2)}) async-start(), calls=%async_computation.8 | async-start | bytes 2293760 | tf_op jit(solution)/shard_map/all_gather | solution.py:45
  406.4 30.1 %all-to-all-start.7 = ((f32[2,32,8,448]{3,1,0,2:T(8,128)}), f32[2,32,8,448]{3,1,0,2:T(8,128)S(1)}, u32[]{:S(2)}, u32[]{:S(2)}) async-start(f32[2,32,8,448]{3,1,0,2:T(8,128)} %copy.68), calls=%async_computation.7 | async-start | bytes 2097152 | tf_op jit(solution)/shard_map/all_to_all | solution.py:49
Sparse Core Ops, SparseCore 0:
  337.9 33.3 all-gather.1
where the time goes:
time: 449 us; the launch traced here: 445 us
  other arithmetic  205 us (46%)
  local copies, waits for them, and re-layouts  84.3 us (19%)
  blocking collectives  76.5 us (17%)
  waiting for transfers between devices  45.2 us (10%)
  starting transfers between devices  20.2 us (4%)
  between operations  14.2 us (3%)
    unnamed x3, other arithmetic  161 us
    unnamed x14, local copies, waits for them, and re-layouts  32.5 us
    all_to_all x1, blocking collectives, per_device(): lax.all_to_all(sectioned, 'fsdp', split_axis=2, concat_axis=2, tiled=True)  31.3 us
    all_to_all x1, blocking collectives, per_device(): lax.all_to_all(going, 'fsdp', split_axis=3, concat_axis=0, tiled=True)  28.5 us
    convert_element_type x1, local copies, waits for them, and re-layouts, per_device(): (block_grouped / block_scales.astype(jnp.float32)[:, :, None]).astype(jnp...  27 us
    all_to_all x1, waiting for transfers between devices, per_device(): lax.all_to_all(going, 'fsdp', split_axis=2, concat_axis=2, tiled=True)  21.7 us
    all_to_all x1, waiting for transfers between devices, per_device(): lax.all_to_all(levels_local, 'replica', split_axis=2, concat_axis=0, tile...  18.3 us
    convert_element_type x1, other arithmetic, dequantise(): integer_levels.astype(jnp.float32).reshape(block_scales.shape + (QBLOCK,))  17.6 us
  transfers between devices with their start and end apart: 6, of which 3 were waited for; matrix products, arithmetic and copies ran while one was open for 60% of the time, Pallas kernels for 0%

commit v1 on v0

--- a/solution.py
+++ b/solution.py
@@ -30,7 +30,15 @@
     group = shard_group_count // replica_count
     piece = momentum.shape[1] // shard_group_count
     levels_owned, scales_owned = (
-        lax.all_to_all(levels_local, "replica", split_axis=2, concat_axis=0, tiled=True),
+        jnp.concatenate(
+            lax.all_to_all(
+                jnp.stack(jnp.split(levels_local, lax.axis_size("replica"), axis=2)),
+                "replica",
+                0,
+                0,
+            ),
+            axis=0,
+        ),
         lax.all_to_all(scales_local, "replica", split_axis=2, concat_axis=0, tiled=True),
     )
     summed = jnp.sum(dequantise(levels_owned, scales_owned), axis=0)

time: 449 us -> 250 us (0.56)
  other arithmetic: 205 us -> 27.7 us
  waiting for transfers between devices: 45.2 us -> 92.8 us
  local copies, waits for them, and re-layouts: 84.3 us -> 45.8 us
  blocking collectives: 76.5 us -> 42.8 us
  starting transfers between devices: 20.2 us -> 25.2 us
    unnamed x3 -> x2, other arithmetic: 161 us -> 3.97 us
    all_to_all x1 -> x0, blocking collectives: 31.3 us -> none  [per_device(): lax.all_to_all(sectioned, 'fsdp', split_axis=2, concat_axis=2, tiled=True)]
    all_to_all x1 -> x2, waiting for transfers between devices: 18.3 us -> 45.3 us  [the longest x1 25.6 us: per_device(): lax.all_to_all(sectioned, 'fsdp', split_axis=2, concat_axis=2, tiled=True)]
    convert_element_type x1 -> x2, local copies, waits for them, and re-layouts: 27 us -> 0.12 us  [dequantise(): values = shaped * block_scales.astype(jnp.float32)[..., None]]
    convert_element_type x3 -> x1, other arithmetic: 17.7 us -> 0.01 us  [per_device(): block_scales.astype(jnp.float32)[:, :, None]]
    unnamed x14 -> x10, local copies, waits for them, and re-layouts: 32.5 us -> 15.1 us
    all_to_all x1, waiting for transfers between devices: 0.01 us -> 15.2 us  [per_device(): lax.all_to_all(sectioned, 'fsdp', split_axis=0, concat_axis=3, tiled=True)]
    mul x0 -> x2, local copies, waits for them, and re-layouts: none -> 7.23 us  [dequantise(): values = shaped * block_scales.astype(jnp.float32)[..., None]]
  transfers between devices with their start and end apart: 6 -> 7, of which waited for: 3 -> 5; matrix products, arithmetic and copies ran while one was open for 60% -> 21% of each run, Pallas kernels for 0% -> 0%
where the time goes in v1:
time: 250 us; the launch traced here: 249 us
  waiting for transfers between devices  92.8 us (37%)
  local copies, waits for them, and re-layouts  45.8 us (18%)
  blocking collectives  42.8 us (17%)
  other arithmetic  27.7 us (11%)
  starting transfers between devices  25.2 us (10%)
  between operations  14.2 us (6%)
    all_to_all x1, blocking collectives, per_device(): lax.all_to_all(going, 'fsdp', split_axis=3, concat_axis=0, tiled=True)  26.2 us
    all_to_all x1, waiting for transfers between devices, per_device(): lax.all_to_all(sectioned, 'fsdp', split_axis=2, concat_axis=2, tiled=True)  25.6 us
    all_to_all x1, waiting for transfers between devices, per_device(): lax.all_to_all(going, 'fsdp', split_axis=2, concat_axis=2, tiled=True)  21.7 us
    all_to_all x1, waiting for transfers between devices, per_device(): lax.all_to_all(jnp.stack(jnp.split(levels_local, lax.axis_size('replica')...  19.7 us
    all_to_all x1, blocking collectives, per_device(): lax.all_to_all(going, 'replica', split_axis=0, concat_axis=2, tiled=True)  16.7 us
    all_to_all x1, waiting for transfers between devices, per_device(): lax.all_to_all(sectioned, 'fsdp', split_axis=0, concat_axis=3, tiled=True)  15.2 us
    unnamed x10, local copies, waits for them, and re-layouts  15.1 us
    all_to_all x1, waiting for transfers between devices, per_device(): lax.all_to_all(sectioned, 'replica', split_axis=2, concat_axis=0, tiled=T...  10.6 us
  transfers between devices with their start and end apart: 7, of which 5 were waited for; matrix products, arithmetic and copies ran while one was open for 21% of the time, Pallas kernels for 0%

profile of v1, /device:TPU:0, one launch (start us, length us, event | category | flops | bytes accessed | tf_op | source)
XLA Modules:
  0.0 248.5 jit_solution(6518958844856643947)
XLA Ops:
  7.2 3.0 %abs_bitcast_fusion = f32[4,8,224,128]{3,1,2,0:T(8,128)S(1)} fusion(f32[32,28672]{1,0:T(8,128)} %param.4, bf16[1,32,28672]{2,1,0:T(8,128)(2,1)} %param.3), kind=kLoop, calls=%fused_computation.5 | loop fusion | flops 2752512 | bytes 9175040
  10.2 2.5 %copy.60 = f32[4,8,224,128]{3,2,1,0:T(8,128)} copy(f32[4,8,224,128]{3,1,2,0:T(8,128)S(1)} %abs_bitcast_fusion) | data formatting | bytes 7340032
  12.6 3.2 %reduce_max.9 = f32[32,224]{1,0:T(8,128)S(1)} reduce(f32[32,224,128]{2,1,0:T(8,128)} %bitcast.61, f32[]{:T(128)} %constant.1.clone.1), dimensions={2}, to_apply=%region_0.0 | reduce | flops 910336 | bytes 3698692 | tf_op jit(solution)/shard_map/reduce_max | solution.py:22
  15.9 0.1 copy.44
  16.0 0.5 broadcast.56
  16.5 1.0 reduce.2
  17.5 0.7 reshape.106
  18.2 5.2 %all-to-all-start.1 = ((bf16[4,2,896]{2,1,0:T(2,128)(2,1)}), bf16[4,2,896]{2,1,0:T(2,128)(2,1)S(1)}, u32[]{:S(2)}, u32[]{:S(2)}) async-start(bf16[4,2,896]{2,1,0:T(2,128)(2,1)} %reshape.106), calls=%async_computation.1 | async-start | bytes 28672 | tf_op jit(solution)/shard_map/all_to_all | solution.py:42
  23.4 0.0 copy-start
  23.4 1.0 div.20
  24.4 1.0 copy-done
  25.4 3.8 %fusion.1 = bf16[1,32,28672]{2,1,0:T(8,128)(2,1)S(1)} fusion(f32[4,8,224,128]{3,2,1,0:T(8,128)S(1)} %bitcast.64, f32[32,28672]{1,0:T(8,128)S(1)} %copy-done, bf16[1,32,28672]{2,1,0:T(8,128)(2,1)} %param.3), kind=kLoop, calls=%fused_computation.7 | loop fusion | flops 3670016 | bytes 11010048 | tf_op jit(solution)/shard_map/convert_element_type | solution.py:23
  29.3 1.7 reshape.101
  30.9 1.6 copy.47
  32.5 0.0 all-to-all-done.1
  32.5 4.9 %all-to-all-start.2 = ((f32[2,32,8,448]{3,1,0,2:T(8,128)}), f32[2,32,8,448]{3,1,0,2:T(8,128)}, u32[]{:S(2)}, u32[]{:S(2)}) async-start(f32[2,32,8,448]{3,1,0,2:T(8,128)} %copy.47), calls=%async_computation.2 | async-start | bytes 2097152 | tf_op jit(solution)/shard_map/all_to_all | solution.py:46
  37.4 1.1 slice_bitcast_fusion.3
  38.5 25.6 %all-to-all-done.2 = f32[2,32,8,448]{3,1,0,2:T(8,128)} async-done(((f32[2,32,8,448]{3,1,0,2:T(8,128)}), f32[2,32,8,448]{3,1,0,2:T(8,128)}, u32[]{:S(2)}, u32[]{:S(2)}) %all-to-all-start.2) | async-done | bytes 917536 | tf_op jit(solution)/shard_map/all_to_all | solution.py:46
  64.1 4.2 %all-to-all-start.3 = ((f32[2,32,8,448]{3,1,0,2:T(8,128)}), f32[2,32,8,448]{3,1,0,2:T(8,128)S(1)}, u32[]{:S(2)}, u32[]{:S(2)}) async-start(f32[2,32,8,448]{3,1,0,2:T(8,128)} %all-to-all-done.2), calls=%async_computation.3 | async-start | bytes 2097152 | tf_op jit(solution)/shard_map/all_to_all | solution.py:47
  68.3 2.8 %pad_maximum_fusion = bf16[4,1,32,7168]{3,2,1,0:T(8,128)(2,1)} fusion(bf16[1,1,32,7168]{3,2,1,0:T(8,128)(2,1)} %get-tuple-element.3, bf16[1,1,32,7168]{3,2,1,0:T(8,128)(2,1)} %get-tuple-element.4, bf16[1,1,32,7168]{3,2,1,0:T(8,128)(2,1)} %get-tuple-element.5, bf16[1,1,32,7168]{3,2,1,0:T(8,128)(2,1)S(1)} %get-tuple-element.2), kind=kLoop, calls=%fused_computation.6 | loop fusion | flops 2752512 | bytes 3670016 | tf_op jit(solution)/shard_map/stack | solution.py:35
  71.0 10.6 %all-to-all-done.3 = f32[2,32,8,448]{3,1,0,2:T(8,128)S(1)} async-done(((f32[2,32,8,448]{3,1,0,2:T(8,128)}), f32[2,32,8,448]{3,1,0,2:T(8,128)S(1)}, u32[]{:S(2)}, u32[]{:S(2)}) %all-to-all-start.3) | async-done | bytes 917536 | tf_op jit(solution)/shard_map/all_to_all | solution.py:47
  81.6 3.6 %all-to-all-start = ((bf16[4,1,32,7168]{3,2,1,0:T(8,128)(2,1)}), bf16[4,1,32,7168]{3,2,1,0:T(8,128)(2,1)S(1)}, u32[]{:S(2)}, u32[]{:S(2)}) async-start(bf16[4,1,32,7168]{3,2,1,0:T(8,128)(2,1)} %pad_maximum_fusion), calls=%async_computation | async-start | bytes 3670016 | tf_op jit(solution)/shard_map/all_to_all | solution.py:34
  85.2 1.8 copy.48
  87.0 19.7 %all-to-all-done = bf16[4,1,32,7168]{3,2,1,0:T(8,128)(2,1)S(1)} async-done(((bf16[4,1,32,7168]{3,2,1,0:T(8,128)(2,1)}), bf16[4,1,32,7168]{3,2,1,0:T(8,128)(2,1)S(1)}, u32[]{:S(2)}, u32[]{:S(2)}) %all-to-all-start) | async-done | bytes 1835040 | tf_op jit(solution)/shard_map/all_to_all | solution.py:34
  106.8 3.6 %all-to-all-start.4 = ((f32[8,32,2,448]{3,2,1,0:T(2,128)}), f32[8,32,2,448]{3,2,1,0:T(2,128)S(1)}, u32[]{:S(2)}, u32[]{:S(2)}) async-start(f32[8,32,2,448]{3,2,1,0:T(2,128)} %bitcast.11), calls=%async_computation.4 | async-start | bytes 2097152 | tf_op jit(solution)/shard_map/all_to_all | solution.py:48
  110.3 0.2 all-gather.2.cloned.1.call-start
  110.5 0.1 reshape.107
  110.7 0.1 copy.45
  110.7 0.1 reshape.105
  110.9 2.4 mul.46
  113.3 4.8 %mul.47 = f32[4,1,32,7168]{3,2,1,0:T(8,128)} reshape(f32[4,32,56,128]{3,2,1,0:T(8,128)} %mul.46) | data formatting | bytes 7340032 | tf_op jit(solution)/shard_map/mul | solution.py:14
  118.1 3.5 %multiply_reduce_fusion = f32[32,7168]{1,0:T(8,128)} fusion(f32[4,1,32,7168]{3,2,1,0:T(8,128)} %mul.47, bf16[4,1,32,7168]{3,2,1,0:T(8,128)(2,1)S(1)} %all-to-all-done), kind=kLoop, calls=%fused_computation.4 | loop fusion | flops 2523136 | bytes 6422528 | tf_op jit(solution)/shard_map/reduce_sum | solution.py:44
  121.6 15.2 %all-to-all-done.4 = f32[8,32,2,448]{3,2,1,0:T(2,128)S(1)} async-done(((f32[8,32,2,448]{3,2,1,0:T(2,128)}), f32[8,32,2,448]{3,2,1,0:T(2,128)S(1)}, u32[]{:S(2)}, u32[]{:S(2)}) %all-to-all-start.4) | async-done | bytes 917536 | tf_op jit(solution)/shard_map/all_to_all | solution.py:48
  136.8 0.5 multiply_bitcast_fusion
  137.4 0.0 copy-start.1
  137.4 0.6 copy.49
  138.0 0.6 copy.50
  138.6 1.3 mul.52
  139.9 0.0 copy-done.1
  139.9 2.1 broadcast_multiply_fusion
  142.1 0.8 div.25
  142.9 0.4 mul.56
  143.3 0.0 all-gather.2.cloned.1.call-update
  143.3 0.2 copy_add_fusion
  143.5 3.6 %copy.52 = f32[1,32,2,3584]{1,2,0,3:T(2,128)} copy(f32[1,32,2,3584]{3,1,2,0:T(8,128)S(1)} %copy_add_fusion) | data formatting | bytes 1835008 | tf_op jit(solution)/shard_map/add | solution.py:51
  147.1 5.3 %reshape.108 = f32[8,1,28672]{2,1,0:T(1,128)S(1)} reshape(f32[3584,1,2,32]{3,2,1,0:T(2,128)} %bitcast.62) | data formatting | bytes 1835008
  152.4 26.2 %all_to_all.87 = f32[8,1,28672]{2,1,0:T(1,128)S(1)} all-to-all(f32[8,1,28672]{2,1,0:T(1,128)S(1)} %reshape.108), channel_id=1, replica_groups=mesh['replica'=4,'fsdp'=8] {'fsdp'}, dimensions={0} | all-to-all | bytes 1835008 | tf_op jit(solution)/shard_map/all_to_all | solution.py:55
  178.5 0.5 broadcast.57
  179.0 2.8 %reduce.3 = f32[8,28672]{1,0:T(8,128)S(1)} reduce(f32[8,1,28672]{2,1,0:T(1,128)S(1)} %all_to_all.87, f32[]{:T(128)} %broadcast.57), dimensions={1}, to_apply=%all_to_all.70.reduce_sub_computation | reduce | bytes 1835012 | tf_op jit(solution)/shard_map/all_to_all | solution.py:55
  181.9 4.9 %reshape.109 = f32[3584,1,2,32]{3,2,1,0:T(2,128)} reshape(f32[8,28672]{1,0:T(8,128)S(1)} %reduce.3) | data formatting | bytes 1835008
  186.8 5.0 %copy.59 = f32[1,32,2,8,448]{4,1,2,3,0:T(8,128)S(1)} copy(f32[1,32,2,8,448]{1,2,4,3,0:T(2,128)} %bitcast.63) | data formatting | bytes 1835008 | tf_op jit(solution)/shard_map/all_to_all | solution.py:55
  191.8 16.7 %all_to_all.88 = f32[8,32,2,448]{3,1,2,0:T(8,128)S(1)} all-to-all(f32[8,32,2,448]{3,1,2,0:T(8,128)S(1)} %bitcast.68), channel_id=1, replica_groups=mesh['replica'=4,'fsdp'=8] {'replica'}, dimensions={0} | all-to-all | bytes 1835008 | tf_op jit(solution)/shard_map/all_to_all | solution.py:56
  208.5 0.1 copy.55
  208.6 1.1 copy.56
  209.7 3.6 %all-to-all-start.7 = ((f32[2,32,8,448]{3,1,0,2:T(8,128)}), f32[2,32,8,448]{3,1,0,2:T(8,128)S(1)}, u32[]{:S(2)}, u32[]{:S(2)}) async-start(f32[2,32,8,448]{3,1,0,2:T(8,128)} %copy.56), calls=%async_computation.7 | async-start | bytes 2097152 | tf_op jit(solution)/shard_map/all_to_all | solution.py:57
  213.2 0.0 all-gather.2.cloned.1.call-done
  213.3 4.8 %convert_subtract_fusion.1 = f32[32,28672]{1,0:T(8,128)} fusion(f32[32,28672]{1,0:T(8,128)} %param.4, bf16[32,28672]{1,0:T(8,128)(2,1)} %all-gather.2.cloned.1.call-done), kind=kLoop, calls=%fused_computation.3 | loop fusion | flops 1835008 | bytes 9175040 | tf_op jit(solution)/shard_map/sub | solution.py:59
  218.0 21.7 %all-to-all-done.7 = f32[2,32,8,448]{3,1,0,2:T(8,128)S(1)} async-done(((f32[2,32,8,448]{3,1,0,2:T(8,128)}), f32[2,32,8,448]{3,1,0,2:T(8,128)S(1)}, u32[]{:S(2)}, u32[]{:S(2)}) %all-to-all-start.7) | async-done | bytes 917536 | tf_op jit(solution)/shard_map/all_to_all | solution.py:57
  239.7 0.6 copy.57
  240.3 1.3 reshape.102
  (2 shorter events, 0.0 us)
Async XLA Ops:
  18.2 14.3 %all-to-all-start.1 = ((bf16[4,2,896]{2,1,0:T(2,128)(2,1)}), bf16[4,2,896]{2,1,0:T(2,128)(2,1)S(1)}, u32[]{:S(2)}, u32[]{:S(2)}) async-start(bf16[4,2,896]{2,1,0:T(2,128)(2,1)} %reshape.106), calls=%async_computation.1 | async-start | bytes 28672 | tf_op jit(solution)/shard_map/all_to_all | solution.py:42
  23.4 2.0 copy-start
  32.5 31.5 %all-to-all-start.2 = ((f32[2,32,8,448]{3,1,0,2:T(8,128)}), f32[2,32,8,448]{3,1,0,2:T(8,128)}, u32[]{:S(2)}, u32[]{:S(2)}) async-start(f32[2,32,8,448]{3,1,0,2:T(8,128)} %copy.47), calls=%async_computation.2 | async-start | bytes 2097152 | tf_op jit(solution)/shard_map/all_to_all | solution.py:46
  64.1 17.5 %all-to-all-start.3 = ((f32[2,32,8,448]{3,1,0,2:T(8,128)}), f32[2,32,8,448]{3,1,0,2:T(8,128)S(1)}, u32[]{:S(2)}, u32[]{:S(2)}) async-start(f32[2,32,8,448]{3,1,0,2:T(8,128)} %all-to-all-done.2), calls=%async_computation.3 | async-start | bytes 2097152 | tf_op jit(solution)/shard_map/all_to_all | solution.py:47
  81.6 25.1 %all-to-all-start = ((bf16[4,1,32,7168]{3,2,1,0:T(8,128)(2,1)}), bf16[4,1,32,7168]{3,2,1,0:T(8,128)(2,1)S(1)}, u32[]{:S(2)}, u32[]{:S(2)}) async-start(bf16[4,1,32,7168]{3,2,1,0:T(8,128)(2,1)} %pad_maximum_fusion), calls=%async_computation | async-start | bytes 3670016 | tf_op jit(solution)/shard_map/all_to_all | solution.py:34
  106.8 30.1 %all-to-all-start.4 = ((f32[8,32,2,448]{3,2,1,0:T(2,128)}), f32[8,32,2,448]{3,2,1,0:T(2,128)S(1)}, u32[]{:S(2)}, u32[]{:S(2)}) async-start(f32[8,32,2,448]{3,2,1,0:T(2,128)} %bitcast.11), calls=%async_computation.4 | async-start | bytes 2097152 | tf_op jit(solution)/shard_map/all_to_all | solution.py:48
  110.3 102.9 %all-gather.2.cloned.1.call-start = ((), (), s32[]{:S(2)}) async-start(), calls=%async_computation.8 | async-start | bytes 2293760 | tf_op jit(solution)/shard_map/all_gather | solution.py:53
  137.4 2.6 %copy-start.1 = (f32[32,7168]{1,0:T(8,128)S(1)}, f32[32,7168]{1,0:T(8,128)}, u32[]{:S(2)}) copy-start(f32[32,7168]{1,0:T(8,128)} %multiply_reduce_fusion) | copy-start | bytes 2752516
  209.7 30.1 %all-to-all-start.7 = ((f32[2,32,8,448]{3,1,0,2:T(8,128)}), f32[2,32,8,448]{3,1,0,2:T(8,128)S(1)}, u32[]{:S(2)}, u32[]{:S(2)}) async-start(f32[2,32,8,448]{3,1,0,2:T(8,128)} %copy.56), calls=%async_computation.7 | async-start | bytes 2097152 | tf_op jit(solution)/shard_map/all_to_all | solution.py:57
Sparse Core Ops, SparseCore 0:
  143.4 30.9 all-gather.1
